TPU v7x, 128 devices: a whole 4x4x4 slice. The times are simulated.
128 devices in a mesh: req: 8 (over x, core), tok: 16 (over y, z).
Axes of the slice: x: 4, y: 4, z: 4, core: 2. Of those that a mesh axis runs over, the one named last changes fastest.
Arguments:
- hidden_in: bfloat16 [8, 2048, 2048], P('req', 'tok'), may hold values from -6 to 6
- attention_gain: bfloat16 [2048], replicated, may hold values from 0.25 to 1.75
- attend_matrix: bfloat16 [2048, 2560], P(None, 'req'), may hold values from -0.125 to 0.125
- merge_matrix: bfloat16 [2048, 2048], P('req'), may hold values from -1 to 1
- feedforward_gain: bfloat16 [2048], replicated, may hold values from 0.25 to 1.75
- gate_matrix: bfloat16 [2048, 8192], P(None, 'tok'), may hold values from -0.125 to 0.125
- up_matrix: bfloat16 [2048, 8192], P(None, 'tok'), may hold values from -0.125 to 0.125
- down_matrix: bfloat16 [8192, 2048], P('tok'), may hold values from -0.0625 to 0.0625
- kv_pool: bfloat16 [8, 48, 2, 128, 256], P('req', 'tok'), may hold values from -320 to 320
- lengths: int32 [8], P('req'), may hold values from 0 to 16384, as said below
- page_table: int32 [8, 16], P('req'), may hold values from 0 to 47, as said below
- free_slots: int32 [8, 16], P('req'), may hold values from 0 to 47, as said below
Outputs:
- layer_output: bfloat16 [8, 2048, 2048], P('req', 'tok')
- updated_pool: bfloat16 [8, 48, 2, 128, 256], P('req', 'tok')
Inputs may be any that keep to these rules, and one draw needn't show every extreme that they name: `lengths`: multiples of 128; in every draw some request has 0 and some has 16384. For each request the entries of its page_table row and of its free_slots row are all distinct slots of its pool. `free_slots`: see page_table.
All inputs are finite; a program needn't handle non-finite values.
Results may differ from a plain program's by a relative error of at most 0.018.
The roundings to bfloat16 on the way count: a program that leaves them out, or rounds other values in their place, can miss the bound.
Values may be sent and summed in bfloat16 or wider, within the bound.
A program may use at most 192 MiB of HBM per device.

v0:
```python
import math

import jax
import jax.numpy as jnp
from jax import lax
from jax.sharding import PartitionSpec as P

HEADS = 32
KV_HEADS = 4
HEAD_DIM = 64
WINDOW = 2048
PAGE = 128
SPAN = 2048


epsilon = 1e-05
rope_base = 10000.0


def rms_scale(matrix, gain):
    values = matrix.astype(jnp.float32)
    inverse = lax.rsqrt(jnp.mean(values * values, axis=-1, keepdims=True) + epsilon)
    return (values * inverse * gain.astype(jnp.float32)).astype(jnp.bfloat16)


def rotate(values, positions):
    half_dim = values.shape[-1] // 2
    frequency = rope_base ** (-2.0 * jnp.arange(half_dim, dtype=jnp.float32) / values.shape[-1])
    angles = positions.astype(jnp.float32)[:, None] * frequency[None, :]
    cosine = jnp.cos(angles)[:, None, :]
    sine_part = jnp.sin(angles)[:, None, :]
    lower_half = values[..., :half_dim]
    upper_half = values[..., half_dim:]
    return jnp.concatenate(
        [
            lower_half * cosine - upper_half * sine_part,
            upper_half * cosine + lower_half * sine_part,
        ],
        axis=-1,
    )


def attend(queries, all_keys, all_values, query_pos, key_pos):
    row_count = queries.shape[0]
    group_size = HEADS // KV_HEADS
    allowed = (
        (key_pos[None, :] >= 0)
        & (key_pos[None, :] <= query_pos[:, None])
        & (key_pos[None, :] > query_pos[:, None] - WINDOW)
    )
    factor = 1.0 / math.sqrt(HEAD_DIM)
    blocks = []
    for head_index in range(KV_HEADS):
        query_block = queries[
            :, head_index * group_size * HEAD_DIM : (head_index + 1) * group_size * HEAD_DIM
        ].reshape(row_count * group_size, HEAD_DIM)
        key_block = all_keys[:, head_index * HEAD_DIM : (head_index + 1) * HEAD_DIM]
        value_block = all_values[:, head_index * HEAD_DIM : (head_index + 1) * HEAD_DIM]
        scores = (
            lax.dot_general(
                query_block, key_block, (((1,), (1,)), ((), ())), preferred_element_type=jnp.float32
            )
            * factor
        )
        scores = jnp.where(allowed[:, None, :], scores.reshape(row_count, group_size, -1), -jnp.inf)
        row_peak = jnp.max(scores, axis=-1, keepdims=True)
        weights = jnp.exp(scores - row_peak)
        row_total = jnp.sum(weights, axis=-1, keepdims=True)
        weighted = jnp.dot(
            weights.astype(jnp.bfloat16).reshape(row_count * group_size, -1),
            value_block,
            preferred_element_type=jnp.float32,
        )
        blocks.append(weighted.reshape(row_count, group_size, HEAD_DIM) / row_total)
    return jnp.concatenate(blocks, axis=1).reshape(row_count, HEADS * HEAD_DIM).astype(jnp.bfloat16)


def shards(
    hidden_in,
    attention_gain,
    attend_matrix,
    merge_matrix,
    feedforward_gain,
    gate_matrix,
    up_matrix,
    down_matrix,
    kv_pool,
    lengths,
    page_table,
    free_slots,
):
    tokens = hidden_in[0]
    tok_rows = tokens.shape[0]
    length = lengths[0]
    tok_index = lax.axis_index("tok")
    query_width = HEADS * HEAD_DIM
    kv_width = KV_HEADS * HEAD_DIM
    normed = rms_scale(tokens, attention_gain)
    projected = jnp.dot(
        normed,
        lax.all_gather(attend_matrix, "req", axis=1, tiled=True),
        preferred_element_type=jnp.float32,
    )
    positions = length + tok_index * tok_rows + jnp.arange(tok_rows, dtype=jnp.int32)
    queries = (
        rotate(projected[:, :query_width].reshape(tok_rows, HEADS, HEAD_DIM), positions)
        .astype(jnp.bfloat16)
        .reshape(tok_rows, query_width)
    )
    new_keys = (
        rotate(
            projected[:, query_width : query_width + kv_width].reshape(
                tok_rows, KV_HEADS, HEAD_DIM
            ),
            positions,
        )
        .astype(jnp.bfloat16)
        .reshape(tok_rows, kv_width)
    )
    new_values = projected[:, query_width + kv_width :].astype(jnp.bfloat16)
    fresh = jnp.stack([new_keys, new_values])
    table = page_table[0]
    pool_local = kv_pool[0]
    slot_count = pool_local.shape[0]
    key_pos = jnp.concatenate(
        [
            length - WINDOW + jnp.arange(WINDOW, dtype=jnp.int32),
            length + jnp.arange(SPAN, dtype=jnp.int32),
        ]
    )
    whole_pool, span_kv = (
        lax.all_gather(pool_local, "tok", axis=0, tiled=True),
        lax.all_gather(fresh, "tok", axis=1, tiled=True),
    )
    window_pages = whole_pool[table]
    window = jnp.transpose(window_pages, (1, 0, 2, 3)).reshape(2, WINDOW, kv_width)
    all_keys = jnp.concatenate([window[0], span_kv[0]], axis=0)
    all_values = jnp.concatenate([window[1], span_kv[1]], axis=0)
    attended = attend(queries, all_keys, all_values, positions, key_pos)
    merged = jnp.dot(
        attended,
        lax.all_gather(merge_matrix, "req", axis=0, tiled=True),
        preferred_element_type=jnp.float32,
    )
    residual = (tokens.astype(jnp.float32) + merged).astype(jnp.bfloat16)
    normed_two = rms_scale(residual, feedforward_gain)
    piece = lax.all_gather(normed_two, "tok", axis=0, tiled=True)
    gate = jnp.dot(piece, gate_matrix, preferred_element_type=jnp.float32)
    lifted = jnp.dot(piece, up_matrix, preferred_element_type=jnp.float32)
    inner = (jax.nn.silu(gate) * lifted).astype(jnp.bfloat16)
    feed_sum = lax.psum_scatter(
        jnp.dot(inner, down_matrix, preferred_element_type=jnp.float32).astype(jnp.bfloat16),
        "tok",
        scatter_dimension=0,
        tiled=True,
    ).astype(jnp.float32)
    output_rows = (residual.astype(jnp.float32) + feed_sum).astype(jnp.bfloat16)
    span_pages = jnp.transpose(span_kv.reshape(2, -1, PAGE, kv_width), (1, 0, 2, 3)).reshape(
        -1, 2 * PAGE * kv_width
    )
    slot_ids = tok_index * slot_count + jnp.arange(slot_count, dtype=jnp.int32)
    hits = free_slots[0][:, None] == slot_ids[None, :]
    placed = jnp.dot(
        hits.T.astype(jnp.bfloat16), span_pages, preferred_element_type=jnp.float32
    ).astype(jnp.bfloat16)
    filled = jnp.any(hits, axis=0)
    new_local = jnp.where(filled[:, None], placed, pool_local.reshape(slot_count, -1)).reshape(
        pool_local.shape
    )
    return (output_rows[None], new_local[None])


def solution(mesh):
    in_specs = (
        P("req", "tok", None),
        P(),
        P(None, "req"),
        P("req", None),
        P(),
        P(None, "tok"),
        P(None, "tok"),
        P("tok", None),
        P("req", "tok", None, None, None),
        P("req"),
        P("req", None),
        P("req", None),
    )
    out_specs = (P("req", "tok", None), P("req", "tok", None, None, None))
    return jax.shard_map(shards, mesh=mesh, in_specs=in_specs, out_specs=out_specs, check_vma=False)
```

profile of v0, /device:TPU:0, one launch (start us, length us, event | category | flops | bytes accessed | tf_op | source)
XLA Modules:
  0.0 495.3 jit_solution(5422393947155966126)
XLA Ops:
  7.2 0.7 all-gather.7.cloned.1.call-update
  8.0 0.7 all-gather.15.cloned.1.call-update
  8.7 0.7 convert_element_type.89
  10.1 1.2 fusion.31
  11.3 0.7 multiply_cosine_fusion
  12.1 58.5 %all-gather.7.cloned.1.call-done = bf16[2048,2560]{0,1:T(8,128)(2,1)} async-done(((bf16[2048,320]{0,1:T(8,128)(2,1)}), bf16[2048,2560]{0,1:T(8,128)(2,1)}) %all-gather.7.cloned.1.call-update) | async-done | bytes 10485776 | tf_op jit(solution)/shard_map/all_gather | solution.py:101
  70.6 7.8 %fusion.98 = f32[128,2560]{1,0:T(8,128)S(1)} fusion(bf16[2048,2560]{0,1:T(8,128)(2,1)} %all-gather.7.cloned.1.call-done, bf16[1,128,2048]{2,1,0:T(8,128)(2,1)} %param.12, f32[2048]{0:T(1024)S(1)} %convert_element_type.89, f32[128]{0:T(128)S(1)} %add_rsqrt_fusion.1), kind=kOutput, calls=%fused_computation.91 | convolution fusion | flops 1343225856 | bytes 12329472 | tf_op jit(solution)/shard_map/dot_general | solution.py:99
  78.4 0.7 slice.102
  79.1 1.0 copy.72
  80.1 0.7 subtract_convert_fusion.1
  80.9 0.1 copy.73
  81.0 0.7 pad_maximum_fusion.5
  81.8 0.5 all-gather.11.cloned.1.call-update
  82.4 0.7 fusion.107
  83.1 1.3 convert_element_type.101
  84.3 1.4 compare_and_fusion
  85.8 48.8 %all-gather.15.cloned.1.call-done = bf16[1,48,2,128,256]{4,3,2,0,1:T(8,128)(2,1)} async-done(((bf16[1,3,2,128,256]{4,3,2,0,1:T(8,128)(2,1)}), bf16[1,48,2,128,256]{4,3,2,0,1:T(8,128)(2,1)}) %all-gather.15.cloned.1.call-update) | async-done | bytes 6291472 | tf_op jit(solution)/shard_map/all_gather | solution.py:132
  134.6 4.8 gather_fusion
  139.4 2.7 fusion.126
  142.1 2.3 slice.97
  144.4 2.6 copy.69
  147.0 1.3 subtract_convert_fusion
  148.3 0.1 pad_maximum_fusion.4
  148.4 0.8 fusion.127
  149.1 0.1 copy.70
  149.2 0.2 reshape.306
  149.4 1.0 copy.77
  150.5 0.9 reshape.309
  151.3 1.0 copy.75
  152.4 0.9 reshape.308
  153.2 1.0 copy.79
  154.3 0.9 reshape.310
  155.2 26.3 %all-gather.9.cloned.1.call-done = bf16[2,2048,256]{2,1,0:T(8,128)(2,1)} async-done(((bf16[2,128,256]{2,1,0:T(8,128)(2,1)}), bf16[2,2048,256]{2,1,0:T(8,128)(2,1)}) %all-gather.9.cloned.1.call-update) | async-done | bytes 2097168 | tf_op jit(solution)/shard_map/all_gather | solution.py:133
  181.5 2.7 slice_bitcast_fusion.1
  184.2 10.5 %fusion.44 = f32[1024,4096]{1,0:T(8,128)} fusion(bf16[1024,64]{1,0:T(8,128)(2,1)} %reshape.309, bf16[2048,256]{1,0:T(8,128)(2,1)S(1)} %bitcast.173, bf16[2048,256]{1,0:T(8,128)(2,1)S(1)} %get-tuple-element.11), kind=kOutput, calls=%fused_computation.65 | convolution fusion | flops 537919488 | bytes 19005440 | tf_op jit(solution)/shard_map/dot_general | solution.py:60
  194.6 8.1 %fusion.50 = f32[1024,4096]{1,0:T(8,128)} fusion(bf16[1024,64]{1,0:T(8,128)(2,1)S(1)} %copy-done.7, bf16[2048,256]{1,0:T(8,128)(2,1)S(1)} %bitcast.174, bf16[2048,256]{1,0:T(8,128)(2,1)S(1)} %get-tuple-element.11), kind=kOutput, calls=%fused_computation.69 | convolution fusion | flops 537919488 | bytes 19005440 | tf_op jit(solution)/shard_map/dot_general | solution.py:60
  202.8 9.3 %fusion.9 = (f32[1024]{0:T(1024)S(1)}, f32[1024,4096]{1,0:T(8,128)}) fusion(pred[128,4096]{1,0:T(8,128)(4,1)S(1)} %copy-done.2, bf16[1024,64]{1,0:T(8,128)(2,1)S(1)} %reshape.306, bf16[2048,256]{1,0:T(8,128)(2,1)S(1)} %bitcast.175, bf16[2048,256]{1,0:T(8,128)(2,1)S(1)} %get-tuple-element.11), kind=kOutput, calls=%fused_computation.19 | convolution fusion | flops 550501376 | bytes 19533824 | tf_op jit(solution)/shard_map/dot_general | solution.py:60
  212.0 28.7 %fusion.1 = (f32[1024]{0:T(1024)S(1)}, f32[1024]{0:T(1024)S(1)}, f32[1024]{0:T(1024)S(1)}, f32[1024]{0:T(1024)S(1)}, f32[1024,4096]{1,0:T(8,128)}) fusion(f32[1024,4096]{1,0:T(8,128)} %get-tuple-element.24, f32[1024]{0:T(1024)S(1)} %get-tuple-element.23, pred[128,4096]{1,0:T(8,128)(4,1)} %compare_and_fusion, f32[1024,4096]{1,0:T(8,128)} %fusion.44, ...), kind=kOutput, calls=%fused_computation.11 | convolution fusion | flops 592441344 | bytes 69881856 | tf_op jit(solution)/shard_map/dot_general | solution.py:60
  240.7 20.6 %fusion.3 = (f32[1024]{0:T(1024)S(1)}, f32[1024]{0:T(1024)S(1)}, f32[1024]{0:T(1024)S(1)}) fusion(f32[1024,4096]{1,0:T(8,128)} %fusion.50, f32[1024]{0:T(1024)S(1)} %get-tuple-element.5, pred[128,4096]{1,0:T(8,128)(4,1)} %compare_and_fusion, f32[1024]{0:T(1024)S(1)} %get-tuple-element.4, f32[1024,4096]{1,0:T(8,128)} %fusion.44, ...), kind=kLoop, calls=%fused_computation.13 | loop fusion | flops 50328576 | bytes 50880512 | tf_op jit(solution)/shard_map/reduce_sum | solution.py:68
  261.3 0.1 div.68
  261.4 0.7 div.65
  262.1 0.7 div.62
  262.9 0.7 div.59
  263.6 9.8 %fusion.62 = bf16[128,8,64]{2,1,0:T(8,128)(2,1)} fusion(bf16[2048,256]{1,0:T(8,128)(2,1)} %get-tuple-element.12, bf16[2048,256]{1,0:T(8,128)(2,1)} %bitcast.186, f32[1024,4096]{1,0:T(8,128)} %get-tuple-element.25, f32[1024]{0:T(1024)S(1)} %get-tuple-element.3, pred[128,4096]{1,0:T(8,128)(4,1)S(1)} %copy-done.3, f32[128,8]{1,0:T(8,128)S(1)} %div.68), kind=kOutput, calls=%fused_computation.83 | convolution fusion | flops 554827776 | bytes 19537920 | tf_op jit(solution)/shard_map/dot_general | solution.py:69
  273.3 9.2 %fusion.72 = bf16[128,8,64]{2,1,0:T(8,128)(2,1)} fusion(bf16[2048,256]{1,0:T(8,128)(2,1)} %bitcast.187, bf16[2048,256]{1,0:T(8,128)(2,1)} %get-tuple-element.12, f32[1024,4096]{1,0:T(8,128)} %fusion.44, f32[1024]{0:T(1024)S(1)} %get-tuple-element.4, pred[128,4096]{1,0:T(8,128)(4,1)S(1)} %copy-done.3, f32[128,8]{1,0:T(8,128)} %div.65), kind=kOutput, calls=%fused_computation.85 | convolution fusion | flops 554827776 | bytes 19537920 | tf_op jit(solution)/shard_map/dot_general | solution.py:69
  282.6 6.5 %fusion.82 = bf16[128,8,64]{2,1,0:T(8,128)(2,1)} fusion(bf16[2048,256]{1,0:T(8,128)(2,1)} %bitcast.188, bf16[2048,256]{1,0:T(8,128)(2,1)} %get-tuple-element.12, f32[1024,4096]{1,0:T(8,128)S(1)} %bitcast.172, f32[1024]{0:T(1024)S(1)} %get-tuple-element.5, pred[128,4096]{1,0:T(8,128)(4,1)S(1)} %copy-done.3, f32[128,8]{1,0:T(8,128)} %div.62), kind=kOutput, calls=%fused_computation.87 | convolution fusion | flops 554827776 | bytes 19537920 | tf_op jit(solution)/shard_map/dot_general | solution.py:69
  289.0 8.6 %fusion.92 = bf16[128,8,64]{2,1,0:T(8,128)(2,1)S(1)} fusion(bf16[2048,256]{1,0:T(8,128)(2,1)} %bitcast.189, bf16[2048,256]{1,0:T(8,128)(2,1)} %get-tuple-element.12, f32[1024,4096]{1,0:T(8,128)} %get-tuple-element.24, f32[1024]{0:T(1024)S(1)} %get-tuple-element.23, pred[128,4096]{1,0:T(8,128)(4,1)S(1)} %copy-done.3, f32[128,8]{1,0:T(8,128)} %div.59), kind=kOutput, calls=%fused_computation.89 | convolution fusion | flops 554827776 | bytes 19537920 | tf_op jit(solution)/shard_map/dot_general | solution.py:69
  297.7 0.3 pad_maximum_fusion.3
  298.0 1.9 copy.81
  299.9 4.9 multiply_reduce_fusion
  304.8 1.0 multiply_convert_fusion.1
  305.8 0.0 reduce-scatter.2.cloned.1.call-start
  305.9 69.4 %all-gather.13.cloned.1.call-done = bf16[2048,2048]{1,0:T(8,128)(2,1)} async-done(((bf16[128,2048]{1,0:T(8,128)(2,1)}), bf16[2048,2048]{1,0:T(8,128)(2,1)}) %all-gather.13.cloned.1.call-update) | async-done | bytes 8388624 | tf_op jit(solution)/shard_map/all_gather | solution.py:147
  375.2 10.5 %fusion.128 = f32[2048,512]{1,0:T(8,128)} fusion(bf16[2048,2048]{1,0:T(8,128)(2,1)} %all-gather.13.cloned.1.call-done, bf16[2048,512]{1,0:T(8,128)(2,1)} %param.17), kind=kOutput, calls=%fused_computation.143 | convolution fusion | flops 4294967296 | bytes 14680064 | tf_op jit(solution)/shard_map/dot_general | solution.py:148
  385.7 14.9 %convolution_convert_fusion.1 = bf16[2048,2048]{1,0:T(8,128)(2,1)} fusion(bf16[512,2048]{1,0:T(8,128)(2,1)S(1)} %copy-done, f32[2048,512]{1,0:T(8,128)} %fusion.128, bf16[2048,2048]{1,0:T(8,128)(2,1)} %all-gather.13.cloned.1.call-done, bf16[2048,512]{1,0:T(8,128)(2,1)} %param.18), kind=kOutput, calls=%fused_computation.35 | convolution fusion | flops 8600420352 | bytes 25165824 | tf_op jit(solution)/shard_map/dot_general | solution.py:152
  400.6 1.0 copy-done.6
  401.6 1.0 reshape_squeeze.3
  402.6 0.2 compare_reduce_fusion
  402.8 1.7 copy.82
  404.5 1.2 copy.91
  405.7 0.7 fusion
  406.4 0.8 copy.92
  407.2 79.0 %reduce-scatter.2.cloned.1.call-done = bf16[128,2048]{1,0:T(8,128)(2,1)} async-done(((bf16[2048,2048]{1,0:T(8,128)(2,1)}), bf16[128,2048]{1,0:T(8,128)(2,1)}) %reduce-scatter.2.cloned.1.call-update) | async-done | bytes 524304 | tf_op jit(solution)/shard_map/reduce_scatter | solution.py:151
  486.3 1.9 fusion.97
  (57 shorter events, 0.4 us)
Async XLA Ops:
  7.2 378.5 %copy-start = (bf16[512,2048]{1,0:T(8,128)(2,1)S(1)}, bf16[512,2048]{1,0:T(8,128)(2,1)}, u32[]{:S(2)}) copy-start(bf16[512,2048]{1,0:T(8,128)(2,1)} %param.19) | copy-start | bytes 6291460
  7.2 63.4 %all-gather.7.cloned.1.call-start = ((), (), s32[]{:S(2)}) async-start(), calls=%async_computation.1 | async-start | bytes 11796480 | tf_op jit(solution)/shard_map/all_gather | solution.py:101
  7.9 126.7 %all-gather.15.cloned.1.call-start = ((), (), s32[]{:S(2)}) async-start(), calls=%async_computation.6 | async-start | bytes 6684672 | tf_op jit(solution)/shard_map/all_gather | solution.py:132
  8.7 172.8 %all-gather.9.cloned.1.call-start = ((), (), s32[]{:S(2)}) async-start(), calls=%async_computation.2 | async-start | bytes 2228224 | tf_op jit(solution)/shard_map/all_gather | solution.py:133
  78.4 61.0 %copy-start.4 = (f32[128,2560]{1,0:T(8,128)}, f32[128,2560]{1,0:T(8,128)S(1)}, u32[]{:S(2)}) copy-start(f32[128,2560]{1,0:T(8,128)S(1)} %fusion.98) | copy-start | bytes 3932164
  81.7 65.3 %copy-start.11 = (f32[128,32]{0,1:T(8,128)S(1)}, f32[128,32]{0,1:T(8,128)}, u32[]{:S(2)}) copy-start(f32[128,32]{0,1:T(8,128)} %get-tuple-element.22) | copy-start | bytes 49156
  81.7 218.1 %all-gather.11.cloned.1.call-start = ((), (), s32[]{:S(2)}) async-start(), calls=%async_computation.3 | async-start | bytes 9437184 | tf_op jit(solution)/shard_map/all_gather | solution.py:142
  82.3 292.9 %all-gather.13.cloned.1.call-start = ((), (), s32[]{:S(2)}) async-start(), calls=%async_computation.4 | async-start | bytes 8912896 | tf_op jit(solution)/shard_map/all_gather | solution.py:147
  184.2 18.6 %copy-start.1 = (bf16[2048,256]{1,0:T(8,128)(2,1)}, bf16[2048,256]{1,0:T(8,128)(2,1)S(1)}, u32[]{:S(2)}) copy-start(bf16[2048,256]{1,0:T(8,128)(2,1)S(1)} %get-tuple-element.11) | copy-start | bytes 3145732
  184.2 10.5 %copy-start.7 = (bf16[1024,64]{1,0:T(8,128)(2,1)S(1)}, bf16[1024,64]{1,0:T(8,128)(2,1)}, u32[]{:S(2)}) copy-start(bf16[1024,64]{1,0:T(8,128)(2,1)} %reshape.308) | copy-start | bytes 393220
  194.6 8.1 %copy-start.2 = (pred[128,4096]{1,0:T(8,128)(4,1)S(1)}, pred[128,4096]{1,0:T(8,128)(4,1)}, u32[]{:S(2)}) copy-start(pred[128,4096]{1,0:T(8,128)(4,1)} %compare_and_fusion) | copy-start | bytes 1572868
  240.7 22.9 %copy-start.3 = (pred[128,4096]{1,0:T(8,128)(4,1)S(1)}, pred[128,4096]{1,0:T(8,128)(4,1)}, u32[]{:S(2)}) copy-start(pred[128,4096]{1,0:T(8,128)(4,1)} %compare_and_fusion) | copy-start | bytes 1572868
  263.6 19.0 %slice-start = ((s8[16777216]{0:T(1024)(128)(4,1)}), s8[4194304]{0:T(1024)(128)(4,1)S(1)}, s32[]{:S(2)}) async-start(s8[16777216]{0:T(1024)(128)(4,1)} %bitcast.171), calls=%async_computation.7 | async-start | bytes 8388608
  263.6 19.0 %slice-start.1 = ((s8[16777216]{0:T(1024)(128)(4,1)}), s8[4194304]{0:T(1024)(128)(4,1)S(1)}, s32[]{:S(2)}) async-start(s8[16777216]{0:T(1024)(128)(4,1)} %bitcast.171), calls=%async_computation.8 | async-start | bytes 8388608
  273.3 9.2 %slice-start.2 = ((s8[16777216]{0:T(1024)(128)(4,1)}), s8[4194304]{0:T(1024)(128)(4,1)S(1)}, s32[]{:S(2)}) async-start(s8[16777216]{0:T(1024)(128)(4,1)} %bitcast.171), calls=%async_computation.9 | async-start | bytes 8388608
  273.3 9.2 %slice-start.3 = ((s8[16777216]{0:T(1024)(128)(4,1)}), s8[4194304]{0:T(1024)(128)(4,1)S(1)}, s32[]{:S(2)}) async-start(s8[16777216]{0:T(1024)(128)(4,1)} %bitcast.171), calls=%async_computation.10 | async-start | bytes 8388608
  289.0 8.7 %copy-start.8 = (bf16[128,8,64]{2,1,0:T(8,128)(2,1)S(1)}, bf16[128,8,64]{2,1,0:T(8,128)(2,1)}, u32[]{:S(2)}) copy-start(bf16[128,8,64]{2,1,0:T(8,128)(2,1)} %fusion.62) | copy-start | bytes 393220
  289.0 8.7 %copy-start.9 = (bf16[128,8,64]{2,1,0:T(8,128)(2,1)S(1)}, bf16[128,8,64]{2,1,0:T(8,128)(2,1)}, u32[]{:S(2)}) copy-start(bf16[128,8,64]{2,1,0:T(8,128)(2,1)} %fusion.72) | copy-start | bytes 393220
  289.0 8.7 %copy-start.10 = (bf16[128,8,64]{2,1,0:T(8,128)(2,1)S(1)}, bf16[128,8,64]{2,1,0:T(8,128)(2,1)}, u32[]{:S(2)}) copy-start(bf16[128,8,64]{2,1,0:T(8,128)(2,1)} %fusion.82) | copy-start | bytes 393220
  299.9 5.0 %copy-start.12 = (f32[2048]{0:T(1024)S(1)}, f32[2048]{0:T(1024)}, u32[]{:S(2)}) copy-start(f32[2048]{0:T(1024)} %convert_element_type.101) | copy-start | bytes 24580
  305.8 180.4 %reduce-scatter.2.cloned.1.call-start = ((), (), s32[]{:S(2)}) async-start(), calls=%async_computation.5 | async-start | bytes 8912896 | tf_op jit(solution)/shard_map/reduce_scatter | solution.py:151
  400.6 1.0 copy-start.6
  400.6 2.0 copy-start.13
  402.6 3.1 copy-start.5
Sparse Core Ops, SparseCore 0:
  9.7 60.9 all-gather.6
  72.8 61.7 all-gather.14
  136.8 44.6 all-gather.8
  183.0 48.8 all-gather.10
  305.9 69.2 all-gather.12
  400.8 85.4 reduce-scatter.1
where the time goes:
time: 503 us; the launch traced here: 495 us
  waiting for transfers between devices  284 us (56%)
  matrix products  129 us (26%)
  local copies, waits for them, and re-layouts  33.4 us (7%)
  other arithmetic  32.9 us (7%)
  between operations  15.3 us (3%)
    reduce_scatter x1, waiting for transfers between devices, shards(): lax.psum_scatter(jnp.dot(inner, down_matrix, preferred_element_type=jnp.f...  79 us
    all_gather x1, waiting for transfers between devices, shards(): piece = lax.all_gather(normed_two, 'tok', axis=0, tiled=True)  69.4 us
    all_gather x1, waiting for transfers between devices, shards(): lax.all_gather(attend_matrix, 'req', axis=1, tiled=True)  58.5 us
    dot_general x4, matrix products, attend(): lax.dot_general(query_block, key_block, (((1,), (1,)), ((), ())), preferr...  56.5 us
    all_gather x1, waiting for transfers between devices, shards(): lax.all_gather(pool_local, 'tok', axis=0, tiled=True)  48.8 us
    dot_general x4, matrix products, attend(): jnp.dot(weights.astype(jnp.bfloat16).reshape(row_count * group_size, -1),...  34.1 us
    all_gather x1, waiting for transfers between devices, shards(): lax.all_gather(fresh, 'tok', axis=1, tiled=True)  26.3 us
    reduce_sum x1, other arithmetic, attend(): row_total = jnp.sum(weights, axis=-1, keepdims=True)  20.6 us
  transfers between devices with their start and end apart: 6, of which 5 were waited for; matrix products, arithmetic and copies ran while one was open for 33% of the time, Pallas kernels for 0%

commit v1 on v0

v1 whole, which is shorter than its diff:
```python
import math

import jax
import jax.numpy as jnp
from jax import lax
from jax.experimental import pallas as pl
from jax.experimental.pallas import tpu as pltpu
from jax.sharding import PartitionSpec as P

HEADS = 32
KV_HEADS = 4
HEAD_DIM = 64
WINDOW = 2048
PAGE = 128
SPAN = 2048
D = 2048
FF_LOCAL = 512
QW = HEADS * HEAD_DIM
KVW = KV_HEADS * HEAD_DIM
WPAGES = WINDOW // PAGE
SEEN = WPAGES + 1
N_TOK = 16

epsilon = 1e-05
rope_base = 10000.0
MASKED = -1e30


def rms_scale(matrix, gain):
    values = matrix.astype(jnp.float32)
    inverse = lax.rsqrt(jnp.mean(values * values, axis=-1, keepdims=True) + epsilon)
    return (values * inverse * gain.astype(jnp.float32)).astype(jnp.bfloat16)


def rope_tables(positions):
    half_dim = HEAD_DIM // 2
    frequency = rope_base ** (-2.0 * jnp.arange(half_dim, dtype=jnp.float32) / HEAD_DIM)
    angles = positions.astype(jnp.float32)[:, None] * frequency[None, :]
    cosine = jnp.cos(angles)
    sine = jnp.sin(angles)
    return (
        jnp.concatenate([cosine] * 4, axis=1),
        jnp.concatenate([-sine, sine, -sine, sine], axis=1),
    )


def rope_slab(slab, cosine, sine):
    lane = lax.broadcasted_iota(jnp.int32, slab.shape, 1)
    swapped = jnp.where(lane % 64 < 32, pltpu.roll(slab, 96, 1), pltpu.roll(slab, 32, 1))
    return slab * cosine + swapped * sine


def attention_kernel(
    table_ref,
    free_ref,
    length_ref,
    proj_ref,
    cos_ref,
    sin_ref,
    pool_ref,
    span_ref,
    local_ref,
    out_ref,
    new_ref,
    kbuf,
    vbuf,
    bias,
    page_sems,
    slot_sems,
):
    t = lax.axis_index("tok")
    slots = new_ref.shape[0]

    def page_copy(g, kv, source):
        target = (kbuf if kv == 0 else vbuf).at[pl.ds(pl.multiple_of(g * PAGE, PAGE), PAGE)]
        return pltpu.make_async_copy(source, target, page_sems.at[g, kv])

    def fetch(g, carry):
        page = t + g

        @pl.when(page < WPAGES)
        def _():
            slot = table_ref[jnp.minimum(page, WPAGES - 1)]
            for kv in range(2):
                page_copy(g, kv, pool_ref.at[slot, kv]).start()

        @pl.when(page >= WPAGES)
        def _():
            rows = pl.ds(pl.multiple_of(jnp.maximum(page - WPAGES, 0) * PAGE, PAGE), PAGE)
            for kv in range(2):
                page_copy(g, kv, span_ref.at[kv, rows]).start()

        return carry

    lax.fori_loop(0, SEEN, fetch, 0)

    for s in range(slots):
        slot_id = t * slots + s
        found = jnp.int32(-1)
        for j in range(N_TOK):
            found = jnp.where(free_ref[j] == slot_id, j, found)

        @pl.when(found >= 0)
        def _():
            rows = pl.ds(pl.multiple_of(jnp.maximum(found, 0) * PAGE, PAGE), PAGE)
            for kv in range(2):
                pltpu.make_async_copy(
                    span_ref.at[kv, rows], new_ref.at[s, kv], slot_sems.at[s, kv]
                ).start()

        @pl.when(found < 0)
        def _():
            for kv in range(2):
                pltpu.make_async_copy(
                    local_ref.at[s, kv], new_ref.at[s, kv], slot_sems.at[s, kv]
                ).start()

    row = lax.broadcasted_iota(jnp.int32, (PAGE, SEEN * PAGE), 0)
    column = lax.broadcasted_iota(jnp.int32, (PAGE, SEEN * PAGE), 1)
    first = jnp.maximum((WINDOW - length_ref[0]) - t * PAGE, 0)
    allowed = (column > row) & (column <= row + WINDOW) & (column >= first)
    bias[...] = jnp.where(allowed, 0.0, MASKED)

    def drain(g, carry):
        for kv in range(2):
            page_copy(g, kv, pool_ref.at[0, kv]).wait()
        return carry

    lax.fori_loop(0, SEEN, drain, 0)

    lane = lax.broadcasted_iota(jnp.int32, (PAGE, 128), 1)
    low = lane < 64
    factor = math.log2(math.e) / math.sqrt(HEAD_DIM)

    def pair_step(pair, carry):
        columns = pl.ds(pl.multiple_of(pair * 128, 128), 128)
        shared = pl.ds(pl.multiple_of((pair // 8) * 128, 128), 128)
        even_group = (pair // 4) % 2 == 0
        slab = rope_slab(proj_ref[:, columns], cos_ref[...], sin_ref[...])
        turned = pltpu.roll(slab, 64, 1)
        query_one = jnp.where(even_group, jnp.where(low, slab, 0.0), jnp.where(low, 0.0, turned))
        query_two = jnp.where(even_group, jnp.where(low, turned, 0.0), jnp.where(low, 0.0, slab))
        both = jnp.concatenate([query_one, query_two], axis=0).astype(jnp.bfloat16)
        scores = lax.dot_general(
            both, kbuf[:, shared], (((1,), (1,)), ((), ())), preferred_element_type=jnp.float32
        )
        scores = scores.reshape(2, PAGE, SEEN * PAGE) * factor + bias[...][None]
        peak = jnp.max(scores, axis=-1, keepdims=True)
        weights = jnp.exp2(scores - peak)
        total = jnp.sum(weights, axis=-1, keepdims=True)
        weighted = jnp.dot(
            weights.astype(jnp.bfloat16).reshape(2 * PAGE, SEEN * PAGE),
            vbuf[:, shared],
            preferred_element_type=jnp.float32,
        ).reshape(2, PAGE, 128)
        weighted = weighted / total
        one, two = weighted[0], weighted[1]
        left = jnp.where(even_group, one, pltpu.roll(one, 64, 1))
        right = jnp.where(even_group, pltpu.roll(two, 64, 1), two)
        out_ref[:, columns] = jnp.where(low, left, right).astype(jnp.bfloat16)
        return carry

    lax.fori_loop(0, HEADS // 2, pair_step, 0)

    for s in range(slots):
        for kv in range(2):
            pltpu.make_async_copy(
                local_ref.at[s, kv], new_ref.at[s, kv], slot_sems.at[s, kv]
            ).wait()


def attention(table, free, length, projected, cosine, sine, pool, span, pool_local):
    vmem = pl.BlockSpec(memory_space=pltpu.VMEM)
    smem = pl.BlockSpec(memory_space=pltpu.SMEM)
    hbm = pl.BlockSpec(memory_space=pl.ANY)
    rows = projected.shape[0]
    return pl.pallas_call(
        attention_kernel,
        name="window_attention",
        out_shape=(
            jax.ShapeDtypeStruct((rows, QW), jnp.bfloat16),
            jax.ShapeDtypeStruct(pool_local.shape, jnp.bfloat16),
        ),
        in_specs=[smem, smem, smem, vmem, vmem, vmem, hbm, hbm, hbm],
        out_specs=(vmem, vmem),
        scratch_shapes=[
            pltpu.VMEM((SEEN * PAGE, KVW), jnp.bfloat16),
            pltpu.VMEM((SEEN * PAGE, KVW), jnp.bfloat16),
            pltpu.VMEM((PAGE, SEEN * PAGE), jnp.float32),
            pltpu.SemaphoreType.DMA((SEEN, 2)),
            pltpu.SemaphoreType.DMA((pool_local.shape[0], 2)),
        ],
        compiler_params=pltpu.CompilerParams(vmem_limit_bytes=40 << 20),
        cost_estimate=pl.CostEstimate(
            flops=4 * rows * HEADS * SEEN * PAGE * 128,
            bytes_accessed=8 << 20,
            transcendentals=rows * HEADS * SEEN * PAGE,
        ),
    )(table, free, length, projected, cosine, sine, pool, span, pool_local)


RINGS = 4
PART = PAGE // RINGS
HALF = D // 2


def ring_neighbours():
    t = lax.axis_index("tok")
    y, z = t // 4, t % 4

    def at(row, column):
        return ((row + 4) % 4) * 4 + (column + 4) % 4

    down_one = jnp.where((z + y) % 4 == 3, at(y + 1, z), at(y, z + 1))
    up_one = jnp.where((z + y) % 4 == 0, at(y - 1, z), at(y, z - 1))
    down_two = jnp.where((z + y) % 4 == 3, at(y, z + 1), at(y + 1, z))
    up_two = jnp.where((z + y) % 4 == 0, at(y, z - 1), at(y - 1, z))
    return (down_one, up_one, down_two, up_two)


def feed_kernel(
    resid_ref,
    gain_ref,
    gate_ref,
    up_ref,
    down_ref,
    out_ref,
    tok,
    inc,
    pout,
    acc,
    tok_send,
    tok_recv,
    sum_send,
    sum_recv,
):
    targets = ring_neighbours()

    def part(r):
        return pl.ds(r * PART, PART)

    def token_copy(k, r):
        return pltpu.make_async_remote_copy(
            src_ref=tok.at[k, part(r)],
            dst_ref=tok.at[k + 1, part(r)],
            send_sem=tok_send.at[k, r],
            recv_sem=tok_recv.at[k, r],
            device_id={"tok": targets[r]},
            device_id_type=pl.DeviceIdType.MESH,
        )

    def sum_copy(k, half, r):
        return pltpu.make_async_remote_copy(
            src_ref=pout.at[k % 2, half, part(r)],
            dst_ref=inc.at[k - 1, half, part(r)],
            send_sem=sum_send.at[k - 1, half, r],
            recv_sem=sum_recv.at[k - 1, half, r],
            device_id={"tok": targets[r]},
            device_id_type=pl.DeviceIdType.MESH,
        )

    barrier = pltpu.get_barrier_semaphore()
    for target in targets:
        pl.semaphore_signal(
            barrier, inc=1, device_id={"tok": target}, device_id_type=pl.DeviceIdType.MESH
        )

    values = resid_ref[...].astype(jnp.float32)
    inverse = lax.rsqrt(jnp.mean(values * values, axis=-1, keepdims=True) + epsilon)
    tok[0] = (values * inverse * gain_ref[...].astype(jnp.float32)).astype(jnp.bfloat16)

    pl.semaphore_wait(barrier, RINGS)
    for r in range(RINGS):
        token_copy(0, r).start()

    def inner_of(k):
        rows = tok[k]
        gate = jnp.dot(rows, gate_ref[...], preferred_element_type=jnp.float32)
        lifted = jnp.dot(rows, up_ref[...], preferred_element_type=jnp.float32)
        return (gate / (1.0 + jnp.exp(-gate)) * lifted).astype(jnp.bfloat16)

    inner = inner_of(0)
    for half in range(2):
        acc[half] = jnp.dot(
            inner, down_ref[:, half * HALF : (half + 1) * HALF], preferred_element_type=jnp.float32
        )

    def step(k, carry):
        for r in range(RINGS):
            token_copy(k - 1, r).wait_recv()

        @pl.when(k < N_TOK - 1)
        def _():
            for r in range(RINGS):
                token_copy(k, r).start()

        inner = inner_of(k)
        for half in range(2):
            term = jnp.dot(
                inner,
                down_ref[:, half * HALF : (half + 1) * HALF],
                preferred_element_type=jnp.float32,
            )

            @pl.when(k > 2)
            def _():
                for r in range(RINGS):
                    sum_copy(k - 2, half, r).wait_send()

            @pl.when(k > 1)
            def _():
                for r in range(RINGS):
                    sum_copy(k - 1, half, r).wait_recv()
                pout[k % 2, half] = (inc[k - 2, half].astype(jnp.float32) + term).astype(
                    jnp.bfloat16
                )

            @pl.when(k == 1)
            def _():
                pout[k % 2, half] = term.astype(jnp.bfloat16)

            for r in range(RINGS):
                sum_copy(k, half, r).start()
        return carry

    lax.fori_loop(1, N_TOK, step, 0)

    last = N_TOK - 1
    for half in range(2):
        columns = slice(half * HALF, (half + 1) * HALF)
        for r in range(RINGS):
            sum_copy(last, half, r).wait_recv()
        feed = inc[last - 1, half].astype(jnp.float32) + acc[half]
        out_ref[:, columns] = (resid_ref[:, columns].astype(jnp.float32) + feed).astype(
            jnp.bfloat16
        )
    for half in range(2):
        for r in range(RINGS):
            sum_copy(last - 1, half, r).wait_send()
            sum_copy(last, half, r).wait_send()

    def drain(k, carry):
        for r in range(RINGS):
            token_copy(k, r).wait_send()
        return carry

    lax.fori_loop(0, N_TOK - 1, drain, 0)


def feed_forward(residual, gain, gate, up, down):
    vmem = pl.BlockSpec(memory_space=pltpu.VMEM)
    rows = residual.shape[0]
    return pl.pallas_call(
        feed_kernel,
        name="ring_feed_forward",
        out_shape=jax.ShapeDtypeStruct((rows, D), jnp.bfloat16),
        in_specs=[vmem] * 5,
        out_specs=vmem,
        scratch_shapes=[
            pltpu.VMEM((N_TOK, PAGE, D), jnp.bfloat16),
            pltpu.VMEM((N_TOK - 1, 2, PAGE, HALF), jnp.bfloat16),
            pltpu.VMEM((2, 2, PAGE, HALF), jnp.bfloat16),
            pltpu.VMEM((2, PAGE, HALF), jnp.float32),
            pltpu.SemaphoreType.DMA((N_TOK - 1, RINGS)),
            pltpu.SemaphoreType.DMA((N_TOK - 1, RINGS)),
            pltpu.SemaphoreType.DMA((N_TOK - 1, 2, RINGS)),
            pltpu.SemaphoreType.DMA((N_TOK - 1, 2, RINGS)),
        ],
        compiler_params=pltpu.CompilerParams(
            collective_id=0, has_side_effects=True, vmem_limit_bytes=48 << 20
        ),
    )(residual, gain.reshape(1, D), gate, up, down)


def rotate_keys(keys, cosine, sine):
    rows = keys.shape[0]
    parts = keys.reshape(rows, KV_HEADS, 2, HEAD_DIM // 2)
    cos = cosine[:, None, : HEAD_DIM // 2]
    sin = sine[:, None, HEAD_DIM // 2 : HEAD_DIM]
    lower, upper = parts[:, :, 0], parts[:, :, 1]
    return jnp.concatenate(
        [lower * cos - upper * sin, upper * cos + lower * sin], axis=-1
    ).reshape(rows, KVW)


def shards(
    hidden_in,
    attention_gain,
    attend_matrix,
    merge_matrix,
    feedforward_gain,
    gate_matrix,
    up_matrix,
    down_matrix,
    kv_pool,
    lengths,
    page_table,
    free_slots,
):
    tokens = hidden_in[0]
    tok_rows = tokens.shape[0]
    tok_index = lax.axis_index("tok")
    normed = rms_scale(tokens, attention_gain)
    projected = jnp.dot(
        normed,
        lax.all_gather(attend_matrix, "req", axis=1, tiled=True),
        preferred_element_type=jnp.float32,
    )
    positions = lengths[0] + tok_index * tok_rows + jnp.arange(tok_rows, dtype=jnp.int32)
    cosine, sine = rope_tables(positions)
    new_keys = rotate_keys(projected[:, QW : QW + KVW], cosine, sine).astype(jnp.bfloat16)
    new_values = projected[:, QW + KVW :].astype(jnp.bfloat16)
    fresh = jnp.stack([new_keys, new_values])
    pool_local = kv_pool[0]
    whole_pool = lax.all_gather(pool_local, "tok", axis=0, tiled=True)
    span_kv = lax.all_gather(fresh, "tok", axis=1, tiled=True)
    attended, new_local = attention(
        page_table[0],
        free_slots[0],
        lengths,
        projected,
        cosine,
        sine,
        whole_pool,
        span_kv,
        pool_local,
    )
    merged = jnp.dot(
        attended,
        lax.all_gather(merge_matrix, "req", axis=0, tiled=True),
        preferred_element_type=jnp.float32,
    )
    residual = (tokens.astype(jnp.float32) + merged).astype(jnp.bfloat16)
    output_rows = feed_forward(residual, feedforward_gain, gate_matrix, up_matrix, down_matrix)
    return (output_rows[None], new_local[None])


def solution(mesh):
    in_specs = (
        P("req", "tok", None),
        P(),
        P(None, "req"),
        P("req", None),
        P(),
        P(None, "tok"),
        P(None, "tok"),
        P("tok", None),
        P("req", "tok", None, None, None),
        P("req"),
        P("req", None),
        P("req", None),
    )
    out_specs = (P("req", "tok", None), P("req", "tok", None, None, None))
    return jax.shard_map(shards, mesh=mesh, in_specs=in_specs, out_specs=out_specs, check_vma=False)
```

time: 503 us -> 345 us (0.69); the launches traced: 495 us -> 345 us
  Pallas kernels: 0 us -> 129 us
  matrix products: 129 us -> 12.6 us
  waiting for transfers between devices: 284 us -> 179 us
  other arithmetic: 32.9 us -> 3.15 us
  local copies, waits for them, and re-layouts: 33.4 us -> 5.57 us
    pallas_call x0 -> x2, Pallas kernels: none -> 129 us  [the longest x1 100 us: feed_forward(): pl.pallas_call(feed_kernel, name='ring_feed_forward', out_shape=jax.Shape...]
    dot_general x11 -> x0, matrix products: 117 us -> none  [the longest x4 56.5 us: attend(): lax.dot_general(query_block, key_block, (((1,), (1,)), ((), ())), preferr...]
    reduce_scatter x1 -> x0, waiting for transfers between devices: 79 us -> none  [shards(): lax.psum_scatter(jnp.dot(inner, down_matrix, preferred_element_type=jnp.f...]
    all_gather x3 -> x2, waiting for transfers between devices: 145 us -> 102 us  [the longest x1 54.4 us: shards(): whole_pool = lax.all_gather(pool_local, 'tok', axis=0, tiled=True)]
    reduce_sum x1 -> x0, other arithmetic: 20.6 us -> none  [attend(): row_total = jnp.sum(weights, axis=-1, keepdims=True)]
    all_gather x1, waiting for transfers between devices: 0.01 us -> 16.7 us  [shards(): lax.all_gather(merge_matrix, 'req', axis=0, tiled=True)]
    slice x10 -> x2, local copies, waits for them, and re-layouts: 13.2 us -> 0.11 us  [shards(): projected[:, QW:QW + KVW]]
  transfers between devices with their start and end apart: 6 -> 4, of which waited for: 5 -> 4; matrix products, arithmetic and copies ran while one was open for 33% -> 3% of each run, Pallas kernels for 0% -> 9%
where the time goes in v1:
time: 345 us
  waiting for transfers between devices  179 us (52%)
  Pallas kernels  129 us (37%)
  between operations  14.6 us (4%)
  matrix products  12.6 us (4%)
  local copies, waits for them, and re-layouts  5.57 us (2%)
    pallas_call x1, Pallas kernels, feed_forward(): pl.pallas_call(feed_kernel, name='ring_feed_forward', out_shape=jax.Shape...  100 us
    all_gather x1, waiting for transfers between devices, shards(): lax.all_gather(attend_matrix, 'req', axis=1, tiled=True)  58.8 us
    all_gather x1, waiting for transfers between devices, shards(): whole_pool = lax.all_gather(pool_local, 'tok', axis=0, tiled=True)  54.4 us
    all_gather x1, waiting for transfers between devices, shards(): span_kv = lax.all_gather(fresh, 'tok', axis=1, tiled=True)  47.4 us
    pallas_call x1, Pallas kernels, attention(): pl.pallas_call(attention_kernel, name='window_attention', out_shape=(jax....  29.4 us
    all_gather x1, waiting for transfers between devices, shards(): lax.all_gather(merge_matrix, 'req', axis=0, tiled=True)  16.7 us
    dot_general x1, matrix products, shards(): jnp.dot(normed, lax.all_gather(attend_matrix, 'req', axis=1, tiled=True),...  7.77 us
  transfers between devices with their start and end apart: 4, of which 4 were waited for; matrix products, arithmetic and copies ran while one was open for 3% of the time, Pallas kernels for 9%

profile of v1, /device:TPU:0, one launch (start us, length us, event | category | flops | bytes accessed | tf_op | source)
XLA Modules:
  0.0 344.8 jit_solution(14080562540003101301)
XLA Ops:
  7.2 0.0 all-gather.6.cloned.1.call-start
  7.2 0.7 all-gather.6.cloned.1.call-update
  7.9 0.0 all-gather.12.cloned.1.call-start
  7.9 0.7 all-gather.12.cloned.1.call-update
  8.6 0.0 all-gather.8.cloned.1.call-start
  9.3 0.7 convert_element_type.37
  10.1 0.3 fusion.10
  10.4 0.1 copy.32
  10.4 0.1 copy.31
  10.5 1.3 fusion.1
  11.8 0.0 copy-start.8
  11.8 0.0 copy-start.2
  11.8 0.0 copy-start.5
  11.8 0.0 copy-start.6
  11.8 58.8 %all-gather.6.cloned.1.call-done = bf16[2048,2560]{0,1:T(8,128)(2,1)} async-done(((bf16[2048,320]{0,1:T(8,128)(2,1)}), bf16[2048,2560]{0,1:T(8,128)(2,1)}) %all-gather.6.cloned.1.call-update) | async-done | bytes 10485776 | tf_op jit(solution)/shard_map/all_gather | solution.py:406
  70.6 7.8 %fusion.4.proj_ref = f32[128,2560]{1,0:T(8,128)S(1)} fusion(bf16[2048,2560]{0,1:T(8,128)(2,1)} %all-gather.6.cloned.1.call-done, bf16[1,128,2048]{2,1,0:T(8,128)(2,1)} %param.12, f32[2048]{0:T(1024)S(1)} %convert_element_type.37, f32[128]{0:T(128)S(1)} %add_rsqrt_fusion), kind=kOutput, calls=%fused_computation.7 | convolution fusion | flops 1343225856 | bytes 12329472 | tf_op jit(solution)/shard_map/dot_general | solution.py:404
  78.4 0.1 copy.29
  78.5 0.1 copy.33
  78.7 0.7 pad_maximum_fusion
  79.3 0.0 all-gather.8.cloned.1.call-update
  79.4 0.0 all-gather.10.cloned.1.call-start
  79.4 0.5 all-gather.10.cloned.1.call-update
  79.9 0.0 copy-done.8
  80.0 0.2 pad_maximum_fusion.1
  80.1 54.4 %all-gather.12.cloned.1.call-done = bf16[1,48,2,128,256]{4,3,2,0,1:T(8,128)(2,1)} async-done(((bf16[1,3,2,128,256]{4,3,2,0,1:T(8,128)(2,1)}), bf16[1,48,2,128,256]{4,3,2,0,1:T(8,128)(2,1)}) %all-gather.12.cloned.1.call-update) | async-done | bytes 6291472 | tf_op jit(solution)/shard_map/all_gather | solution.py:415
  134.5 47.4 %all-gather.8.cloned.1.call-done.span_ref = bf16[2,2048,256]{2,1,0:T(8,128)(2,1)} async-done(((bf16[2,128,256]{2,1,0:T(8,128)(2,1)}), bf16[2,2048,256]{2,1,0:T(8,128)(2,1)}) %all-gather.8.cloned.1.call-update) | async-done | bytes 2097168 | tf_op jit(solution)/shard_map/all_gather | solution.py:416
  182.0 0.0 copy-done.2
  182.0 0.0 copy-done.5
  182.0 0.0 copy-done.6
  182.0 0.0 copy-start.3
  182.0 2.8 copy-done.3
  184.8 0.0 copy-start.4
  184.8 1.6 copy-done.4
  186.4 0.0 copy-start.7
  186.4 29.4 %window_attention.1 = (bf16[128,2048]{1,0:T(8,128)(2,1)S(1)}, bf16[3,2,128,256]{3,2,1,0:T(8,128)(2,1)}) custom-call(s32[16]{0:T(128)S(1)} %bitcast.42, s32[16]{0:T(128)S(1)} %bitcast.43, s32[1]{0:T(128)} %copy.36.length_ref, f32[128,2560]{1,0:T(8,128)S(1)} %fusion.4.proj_ref, f32[128,128]{1,0:T(8,128)S(1)} %get-tuple-element.11.cos_ref, ...), custom_call_target="tpu_custom_call" | custom-call | flops 4563402752 | bytes 8388608 | tf_op jit(solution)/shard_map/window_attention/pallas_call | solution.py:177
  215.7 16.7 %all-gather.10.cloned.1.call-done = bf16[2048,2048]{1,0:T(8,128)(2,1)} async-done(((bf16[256,2048]{1,0:T(8,128)(2,1)}), bf16[2048,2048]{1,0:T(8,128)(2,1)}) %all-gather.10.cloned.1.call-update) | async-done | bytes 8388624 | tf_op jit(solution)/shard_map/all_gather | solution.py:430
  232.5 0.0 copy-done.7
  232.5 0.0 copy-start
  232.5 0.0 copy-start.1
  232.5 4.8 %fusion.resid_ref = bf16[128,2048]{1,0:T(8,128)(2,1)S(1)} fusion(bf16[128,2048]{1,0:T(8,128)(2,1)S(1)} %get-tuple-element.4, bf16[2048,2048]{1,0:T(8,128)(2,1)} %all-gather.10.cloned.1.call-done, bf16[1,128,2048]{2,1,0:T(8,128)(2,1)S(1)} %copy-done.7), kind=kOutput, calls=%fused_computation.1 | convolution fusion | flops 1074528256 | bytes 9961472 | tf_op jit(solution)/shard_map/dot_general | solution.py:428
  237.3 0.0 copy-done
  237.3 0.0 copy-done.1
  237.3 100.1 %ring_feed_forward.1 = bf16[128,2048]{1,0:T(8,128)(2,1)S(1)} custom-call(bf16[128,2048]{1,0:T(8,128)(2,1)S(1)} %fusion.resid_ref, bf16[1,2048]{1,0:T(2,128)(2,1)S(1)} %reshape.91.gain_ref, bf16[2048,512]{1,0:T(8,128)(2,1)S(1)} %copy-done, bf16[2048,512]{1,0:T(8,128)(2,1)S(1)} %copy-done.1, bf16[512,2048]{1,0:T(8,128)(2,1)} %down_ref.1), custom_call_target="tpu_custom_call" | custom-call | tf_op jit(solution)/shard_map/ring_feed_forward/pallas_call | solution.py:353
  337.4 0.8 copy.37
  (8 shorter events, 0.1 us)
Async XLA Ops:
  7.2 63.4 %all-gather.6.cloned.1.call-start = ((), (), s32[]{:S(2)}) async-start(), calls=%async_computation | async-start | bytes 11796480 | tf_op jit(solution)/shard_map/all_gather | solution.py:406
  7.9 126.6 %all-gather.12.cloned.1.call-start = ((), (), s32[]{:S(2)}) async-start(), calls=%async_computation.3 | async-start | bytes 6684672 | tf_op jit(solution)/shard_map/all_gather | solution.py:415
  8.6 173.3 %all-gather.8.cloned.1.call-start = ((), (), s32[]{:S(2)}) async-start(), calls=%async_computation.1 | async-start | bytes 2228224 | tf_op jit(solution)/shard_map/all_gather | solution.py:416
  11.8 68.2 %copy-start.8 = (bf16[2048]{0:T(1024)(128)(2,1)S(1)}, bf16[2048]{0:T(1024)(128)(2,1)}, u32[]{:S(2)}) copy-start(bf16[2048]{0:T(1024)(128)(2,1)} %param.16) | copy-start | bytes 12292
  11.8 170.2 %copy-start.2 = (bf16[1,3,2,128,256]{4,3,2,1,0:T(8,128)(2,1)S(1)}, bf16[1,3,2,128,256]{4,3,2,1,0:T(8,128)(2,1)}, u32[]{:S(2)}) copy-start(bf16[1,3,2,128,256]{4,3,2,1,0:T(8,128)(2,1)} %param.20) | copy-start | bytes 1179652
  11.8 170.2 %copy-start.5 = (s32[1,16]{1,0:T(1,128)S(1)}, s32[1,16]{1,0:T(1,128)}, u32[]{:S(2)}) copy-start(s32[1,16]{1,0:T(1,128)} %param.22) | copy-start | bytes 196
  11.8 170.2 %copy-start.6 = (s32[1,16]{1,0:T(1,128)S(1)}, s32[1,16]{1,0:T(1,128)}, u32[]{:S(2)}) copy-start(s32[1,16]{1,0:T(1,128)} %param.23) | copy-start | bytes 196
  79.4 153.1 %all-gather.10.cloned.1.call-start = ((), (), s32[]{:S(2)}) async-start(), calls=%async_computation.2 | async-start | bytes 9437184 | tf_op jit(solution)/shard_map/all_gather | solution.py:430
  182.0 2.8 copy-start.3
  184.8 1.6 copy-start.4
  186.4 46.1 %copy-start.7 = (bf16[1,128,2048]{2,1,0:T(8,128)(2,1)S(1)}, bf16[1,128,2048]{2,1,0:T(8,128)(2,1)}, u32[]{:S(2)}) copy-start(bf16[1,128,2048]{2,1,0:T(8,128)(2,1)} %param.12) | copy-start | bytes 1572868
  232.5 4.8 %copy-start = (bf16[2048,512]{1,0:T(8,128)(2,1)S(1)}, bf16[2048,512]{1,0:T(8,128)(2,1)}, u32[]{:S(2)}) copy-start(bf16[2048,512]{1,0:T(8,128)(2,1)} %gate_ref.1) | copy-start | bytes 6291460
  232.5 4.8 %copy-start.1 = (bf16[2048,512]{1,0:T(8,128)(2,1)S(1)}, bf16[2048,512]{1,0:T(8,128)(2,1)}, u32[]{:S(2)}) copy-start(bf16[2048,512]{1,0:T(8,128)(2,1)} %up_ref.1) | copy-start | bytes 6291460
Sparse Core Ops, SparseCore 0:
  9.7 60.9 all-gather.5
  72.8 61.6 all-gather.11
  137.3 44.6 all-gather.7
  183.5 48.8 all-gather.9
